TPU v7x, 32 devices: a whole 2x2x4 slice. The times are simulated.
32 devices in a mesh: tm: 4 (over y, x), space: 8 (over z, core).
Axes of the slice: x: 2, y: 2, z: 4, core: 2. Of those that a mesh axis runs over, the one named last changes fastest.
Arguments:
- signal: bfloat16 [16, 256, 512], P('space', None, 'tm'), may hold values from -6 to 6
- source_boxes: int32 [16, 12], replicated, may hold values from 0 to 15
- near_boxes: int32 [16, 8], replicated, may hold values from 0 to 15, as said below
- trans_kernel: float32 [12, 256, 128], P(None, 'space'), may hold values from -0.15625 to 0.15625
- near_kernel: float32 [8, 128], replicated, may hold values from -0.1875 to 0.1875
Outputs:
- field: bfloat16 [16, 256, 512], P('space', None, 'tm')
Inputs may be any that keep to these rules, and one draw needn't show every extreme that they name: Each near_boxes[b, j] lies within 2 of b.
All inputs are finite; a program needn't handle non-finite values.
Results may differ from a plain program's by a relative error of at most 0.008.
Values may be sent and summed in bfloat16 or wider, within the bound.
A program may use at most 192 MiB of HBM per device.

v0:
```python
import functools

import jax
import jax.numpy as jnp
from jax import lax
from jax.experimental import pallas as pl
from jax.experimental.pallas import tpu as pltpu
from jax.sharding import PartitionSpec as P

REACH = 2
MESH = pl.DeviceIdType.MESH
LANES = 128
SUBLANES = 8
def from_behind(shard, axis, by):
    size = lax.axis_size(axis)
    pairs = [(i, i + by) for i in range(size) if 0 <= i + by < size]
    return lax.ppermute(shard, axis, pairs)


def with_halo(block, sides, width):
    for axis, dim in sides:
        count = lax.axis_size(axis)
        forward = [(i, i + 1) for i in range(count - 1)]
        backward = [(target, source) for source, target in forward]
        low = lax.ppermute(
            lax.slice_in_dim(block, block.shape[dim] - width, None, axis=dim), axis, forward
        )
        high = lax.ppermute(lax.slice_in_dim(block, 0, width, axis=dim), axis, backward)
        block = jnp.concatenate([low, block, high], axis=dim)
    return block


def block_matrix(kernel):
    blocklen = kernel.shape[-1]
    leading = kernel.shape[:-1]
    zeroes = jnp.zeros(leading + (2 * blocklen,), jnp.bfloat16)
    widened = jnp.concatenate([zeroes, kernel.astype(jnp.bfloat16)], axis=-1)
    tiled = jnp.tile(widened, (1,) * len(leading) + (2 * blocklen,))
    trimmed = tiled[..., : 2 * blocklen * (3 * blocklen - 1)]
    skewed = trimmed.reshape(leading + (2 * blocklen, 3 * blocklen - 1))
    return skewed[..., :blocklen]


def body(signal, source_boxes, near_boxes, trans_kernel, near_kernel):
    box_dev = signal.shape[0]
    current_rays = lax.all_to_all(signal, "space", split_axis=1, concat_axis=0, tiled=True)
    earlier_rays = from_behind(current_rays, "tm", 1)
    pair_rays = jnp.concatenate([earlier_rays, current_rays], axis=-1)
    offsets = source_boxes.shape[1]
    far = jnp.zeros(current_rays.shape, jnp.float32)
    for offset in range(offsets):
        trans_mats = block_matrix(trans_kernel[offset])
        rows = jnp.take(pair_rays, source_boxes[:, offset], axis=0)
        far = far + jnp.einsum("brs,rst->brt", rows, trans_mats, preferred_element_type=jnp.float32)
    far_rays = far.astype(jnp.bfloat16)
    near_mats = block_matrix(near_kernel)
    slots = near_boxes.shape[1]
    earlier_box = from_behind(signal, "tm", 1)
    pair_box = jnp.concatenate([earlier_box, signal], axis=-1)
    padded = with_halo(pair_box, (("space", 0),), REACH)
    first = lax.axis_index("space") * box_dev
    own_near = lax.dynamic_slice_in_dim(near_boxes, first, box_dev, 0)
    local_rows = own_near - (first - REACH)
    near_sum = jnp.zeros(signal.shape, jnp.float32)
    for slot in range(slots):
        rows = jnp.take(padded, local_rows[:, slot], axis=0)
        near_sum = near_sum + jnp.einsum(
            "brs,st->brt", rows, near_mats[slot], preferred_element_type=jnp.float32
        )
    near_box = near_sum.astype(jnp.bfloat16)
    far_box = lax.all_to_all(far_rays, "space", split_axis=0, concat_axis=1, tiled=True)
    return (far_box.astype(jnp.float32) + near_box.astype(jnp.float32)).astype(jnp.bfloat16)


def fused_kernel(
    n_tm,
    n_space,
    signal_ref,
    source_ref,
    near_ref,
    trans_ref,
    kernel_ref,
    out_ref,
    staged,
    landed,
    wide,
    trans_rows,
    near_rows,
    trans_mats,
    near_mats,
    far_all,
    near_all,
    leaving,
    sources,
    nears,
    in_send,
    in_recv,
    out_send,
    out_recv,
    local_sem,
    stage_sem,
):
    tm, space = lax.axis_index("tm"), lax.axis_index("space")
    peers = n_tm * n_space
    box_dev = signal_ref.shape[0]
    boxes = n_space * box_dev
    offsets = trans_ref.shape[0]
    slots = kernel_ref.shape[0]
    rows = n_tm * boxes
    block_rows = boxes * SUBLANES

    def wrapped(value, size):
        return jnp.where(value >= size, value - size, value)

    others = [
        (wrapped(tm + dt, n_tm), wrapped(space + ds, n_space))
        for ds in range(n_space)
        for dt in range(n_tm)
        if dt or ds
    ]
    mine = space * n_tm + tm
    own_boxes = pl.ds(space * box_dev, box_dev)

    barrier = pltpu.get_barrier_semaphore()
    for other in others:
        pl.semaphore_signal(barrier, inc=1, device_id=other, device_id_type=MESH)
    first_ray = pl.multiple_of(tm * SUBLANES, SUBLANES)
    fetches = [
        pltpu.make_async_copy(
            trans_ref.at[:, pl.ds(first_ray, SUBLANES), :], trans_rows, local_sem.at[0]
        ),
        pltpu.make_async_copy(kernel_ref, near_rows, local_sem.at[1]),
        pltpu.make_async_copy(source_ref, sources, local_sem.at[2]),
        pltpu.make_async_copy(near_ref, nears, local_sem.at[3]),
    ]
    stagings = [
        pltpu.make_async_copy(signal_ref.at[nth], staged.at[:, nth], stage_sem.at[nth])
        for nth in range(box_dev)
    ]
    for fetch in stagings + fetches:
        fetch.start()
    pltpu.make_async_copy(signal_ref.at[:, mine], landed.at[tm + 1, own_boxes], in_recv).start()
    for staging in stagings:
        staging.wait()
    pl.semaphore_wait(barrier, peers - 1)
    for other in others:
        pltpu.make_async_remote_copy(
            src_ref=staged.at[other[1] * n_tm + other[0]],
            dst_ref=landed.at[tm + 1, own_boxes],
            send_sem=in_send,
            recv_sem=in_recv,
            device_id=other,
            device_id_type=MESH,
        ).start()

    lag = lax.broadcasted_iota(jnp.int32, (LANES, LANES), 1) - lax.broadcasted_iota(
        jnp.int32, (LANES, LANES), 0
    )
    causal = lag >= 0

    def split_rows(response):
        spread = jnp.broadcast_to(response, (LANES, LANES))
        turned = pltpu.roll(spread, 0, 1, stride=1, stride_axis=0)
        now = jnp.where(causal, turned, 0.0).astype(jnp.bfloat16)
        before = jnp.where(causal, 0.0, turned).astype(jnp.bfloat16)
        return before, now

    for fetch in fetches:
        fetch.wait()

    def build(offset, carry):
        responses = trans_rows[offset]
        column = pl.ds(pl.multiple_of(offset * LANES, LANES), LANES)
        for ray in range(SUBLANES):
            before, now = split_rows(responses[ray : ray + 1, :])
            trans_mats[ray, 0:LANES, column] = before
            trans_mats[ray, LANES : 2 * LANES, column] = now
        return carry

    lax.fori_loop(0, offsets, build, 0)
    for slot in range(slots):
        before, now = split_rows(near_rows[slot : slot + 1, :])
        near_mats[0:LANES, slot * LANES : (slot + 1) * LANES] = before
        near_mats[LANES : 2 * LANES, slot * LANES : (slot + 1) * LANES] = now
    wide[0:block_rows, :] = jnp.zeros((block_rows, LANES), jnp.float32)

    arrived = landed.at[pl.ds(1, n_tm)]
    pltpu.make_async_copy(arrived, arrived, in_recv).wait()

    for block in range(1, n_tm + 1):
        wide[block * block_rows : (block + 1) * block_rows, :] = (
            landed[block].astype(jnp.float32).reshape(block_rows, LANES)
        )

    far_rows = far_all.reshape(offsets, rows * SUBLANES, LANES)
    for ray in range(SUBLANES):
        blocks = wide[pl.ds(ray, rows + boxes, stride=SUBLANES), :].astype(jnp.bfloat16)
        pair = jnp.concatenate([blocks[:rows], blocks[boxes:]], axis=1)
        products = jnp.dot(pair, trans_mats[ray], preferred_element_type=jnp.float32)
        for offset in range(offsets):
            far_rows[offset, pl.ds(ray, rows, stride=SUBLANES), :] = products[
                :, offset * LANES : (offset + 1) * LANES
            ]

    for block in range(n_tm):
        low = block * block_rows
        pair = jnp.concatenate(
            [
                wide[low : low + block_rows, :].astype(jnp.bfloat16),
                wide[low + block_rows : low + 2 * block_rows, :].astype(jnp.bfloat16),
            ],
            axis=1,
        )
        products = jnp.dot(pair, near_mats[...], preferred_element_type=jnp.float32)
        for slot in range(slots):
            near_all[slot, block * boxes : (block + 1) * boxes] = products[
                :, slot * LANES : (slot + 1) * LANES
            ].reshape(boxes, SUBLANES, LANES)

    def selected(all_ref, table, count, box, block, by_slot):
        total = None
        for entry in range(count):
            origin = table[entry, box] if by_slot else table[box, entry]
            term = all_ref[entry, origin + block * boxes]
            total = term if total is None else total + term
        return total.astype(jnp.bfloat16).astype(jnp.float32)

    def finish(to_space):
        for nth in range(box_dev):
            box = to_space * box_dev + nth
            for block in range(n_tm):
                far = selected(far_all, sources, offsets, box, block, False)
                near = selected(near_all, nears, slots, box, block, True)
                leaving[block, box] = (far + near).astype(jnp.bfloat16)

    def dispatch(ds):
        to_space = wrapped(space + ds, n_space)
        to_boxes = pl.ds(to_space * box_dev, box_dev)
        for dt in range(n_tm):
            to_tm = wrapped(tm + dt, n_tm)
            if dt or ds:
                pltpu.make_async_remote_copy(
                    src_ref=leaving.at[to_tm, to_boxes],
                    dst_ref=out_ref.at[mine],
                    send_sem=out_send,
                    recv_sem=out_recv,
                    device_id=(to_tm, to_space),
                    device_id_type=MESH,
                ).start()
            else:
                pltpu.make_async_copy(
                    leaving.at[tm, to_boxes], out_ref.at[mine], out_recv
                ).start()

    order = sorted(range(n_space), key=lambda ds: -min(ds, n_space - ds))
    for nth, ds in enumerate(order):
        finish(wrapped(space + ds, n_space))
        if nth:
            dispatch(order[nth - 1])
    dispatch(order[-1])

    sent = staged.at[pl.ds(0, peers - 1)]
    pltpu.make_async_copy(sent, sent, in_send).wait()
    pltpu.make_async_copy(out_ref, out_ref, out_recv).wait()
    pltpu.make_async_copy(sent, sent, out_send).wait()


def fused_body(signal, source_boxes, near_boxes, trans_kernel, near_kernel):
    n_tm, n_space = lax.axis_size("tm"), lax.axis_size("space")
    peers = n_tm * n_space
    box_dev, rays, samples = signal.shape
    boxes = box_dev * n_space
    offsets, slots = trans_kernel.shape[0], near_kernel.shape[0]
    rows = n_tm * boxes
    grouped = signal.reshape(box_dev, peers, SUBLANES, samples)
    hbm = pl.BlockSpec(memory_space=pltpu.HBM)
    field = pl.pallas_call(
        functools.partial(fused_kernel, n_tm, n_space),
        out_shape=jax.ShapeDtypeStruct((peers, box_dev, SUBLANES, samples), jnp.bfloat16),
        in_specs=[hbm] * 5,
        out_specs=pl.BlockSpec(memory_space=pl.ANY),
        scratch_shapes=[
            pltpu.VMEM((peers, box_dev, SUBLANES, LANES), jnp.bfloat16),
            pltpu.VMEM((n_tm + 1, boxes, SUBLANES, LANES), jnp.bfloat16),
            pltpu.VMEM(((rows + boxes) * SUBLANES, LANES), jnp.float32),
            pltpu.VMEM((offsets, SUBLANES, LANES), jnp.float32),
            pltpu.VMEM((slots, LANES), jnp.float32),
            pltpu.VMEM((SUBLANES, 2 * LANES, offsets * LANES), jnp.bfloat16),
            pltpu.VMEM((2 * LANES, slots * LANES), jnp.bfloat16),
            pltpu.VMEM((offsets, rows, SUBLANES, LANES), jnp.float32),
            pltpu.VMEM((slots, rows, SUBLANES, LANES), jnp.float32),
            pltpu.VMEM((n_tm, boxes, SUBLANES, LANES), jnp.bfloat16),
            pltpu.SMEM(source_boxes.shape, jnp.int32),
            pltpu.SMEM(near_boxes.shape[::-1], jnp.int32),
            pltpu.SemaphoreType.DMA,
            pltpu.SemaphoreType.DMA,
            pltpu.SemaphoreType.DMA,
            pltpu.SemaphoreType.DMA,
            pltpu.SemaphoreType.DMA((4,)),
            pltpu.SemaphoreType.DMA((box_dev,)),
        ],
        compiler_params=pltpu.CompilerParams(
            collective_id=0, has_side_effects=True, vmem_limit_bytes=67043328
        ),
    )(grouped, source_boxes, near_boxes.T, trans_kernel, near_kernel)
    return field.transpose(1, 0, 2, 3).reshape(signal.shape)


def routed(signal, source_boxes, near_boxes, trans_kernel, near_kernel):
    n_tm, n_space = lax.axis_size("tm"), lax.axis_size("space")
    box_dev, rays, samples = signal.shape
    rows = n_tm * n_space * box_dev
    fits = rays == n_tm * n_space * SUBLANES and samples == LANES and rows <= 2 * LANES
    chosen = fused_body if fits else body
    return chosen(signal, source_boxes, near_boxes, trans_kernel, near_kernel)


def solution(mesh):
    in_specs = (P("space", None, "tm"), P(), P(), P(None, "space", None), P())
    out_specs = P("space", None, "tm")
    return jax.shard_map(
        routed, mesh=mesh, in_specs=in_specs, out_specs=out_specs, check_vma=False
    )
```

profile of v0, /device:TPU:0, one launch (start us, length us, event | category | flops | bytes accessed | tf_op | source)
XLA Modules:
  0.0 22.0 jit_solution(4056472685055497858)
XLA Ops:
  0.0 20.4 %shard_map.55 = bf16[32,2,8,128]{3,2,1,0:T(8,128)(2,1)} custom-call(bf16[2,32,8,128]{3,2,1,0:T(8,128)(2,1)} %bitcast.7, s32[16,12]{1,0:T(8,128)} %source_ref.1, s32[8,16]{1,0:T(8,128)} %bitcast.8, f32[12,32,128]{2,1,0:T(8,128)} %trans_ref.1, f32[8,128]{1,0:T(8,128)} %kernel_ref.1), custom_call_target="tpu_custom_call" | custom-call | tf_op jit(solution)/shard_map/pallas_call | solution.py:277
  20.4 1.6 %copy_bitcast_fusion = bf16[2,256,128]{2,1,0:T(8,128)(2,1)} fusion(bf16[32,2,8,128]{3,2,1,0:T(8,128)(2,1)} %shard_map.55), kind=kLoop, calls=%fused_computation | loop fusion | bytes 262144 | tf_op jit(solution)/shard_map/reshape | solution.py:306
where the time goes:
time: 22.2 us; the launch traced here: 22 us
  Pallas kernels  20.4 us (92%)
  local copies, waits for them, and re-layouts  1.58 us (7%)
    pallas_call x1, Pallas kernels, fused_body(): pl.pallas_call(functools.partial(fused_kernel, n_tm, n_space), out_shape=...  20.4 us
    reshape x1, local copies, waits for them, and re-layouts, fused_body(): return field.transpose(1, 0, 2, 3).reshape(signal.shape)  1.58 us

commit v1 on v0

--- a/solution.py
+++ b/solution.py
@@ -84,6 +84,7 @@
     staged,
     landed,
     wide,
+    flat,
     trans_rows,
     near_rows,
     trans_mats,
@@ -112,18 +113,16 @@
     def wrapped(value, size):
         return jnp.where(value >= size, value - size, value)
 
+    order = sorted(range(n_space), key=lambda ds: -min(ds, n_space - ds))
     others = [
         (wrapped(tm + dt, n_tm), wrapped(space + ds, n_space))
-        for ds in range(n_space)
-        for dt in range(n_tm)
+        for ds in order
+        for dt in reversed(range(n_tm))
         if dt or ds
     ]
     mine = space * n_tm + tm
     own_boxes = pl.ds(space * box_dev, box_dev)
 
-    barrier = pltpu.get_barrier_semaphore()
-    for other in others:
-        pl.semaphore_signal(barrier, inc=1, device_id=other, device_id_type=MESH)
     first_ray = pl.multiple_of(tm * SUBLANES, SUBLANES)
     fetches = [
         pltpu.make_async_copy(
@@ -137,7 +136,12 @@
         pltpu.make_async_copy(signal_ref.at[nth], staged.at[:, nth], stage_sem.at[nth])
         for nth in range(box_dev)
     ]
-    for fetch in stagings + fetches:
+    for fetch in stagings:
+        fetch.start()
+    barrier = pltpu.get_barrier_semaphore()
+    for other in others:
+        pl.semaphore_signal(barrier, inc=1, device_id=other, device_id_type=MESH)
+    for fetch in fetches:
         fetch.start()
     pltpu.make_async_copy(signal_ref.at[:, mine], landed.at[tm + 1, own_boxes], in_recv).start()
     for staging in stagings:
@@ -183,14 +187,15 @@
         near_mats[0:LANES, slot * LANES : (slot + 1) * LANES] = before
         near_mats[LANES : 2 * LANES, slot * LANES : (slot + 1) * LANES] = now
     wide[0:block_rows, :] = jnp.zeros((block_rows, LANES), jnp.float32)
+    flat[0:block_rows, :] = jnp.zeros((block_rows, LANES), jnp.bfloat16)
 
     arrived = landed.at[pl.ds(1, n_tm)]
     pltpu.make_async_copy(arrived, arrived, in_recv).wait()
 
     for block in range(1, n_tm + 1):
-        wide[block * block_rows : (block + 1) * block_rows, :] = (
-            landed[block].astype(jnp.float32).reshape(block_rows, LANES)
-        )
+        these = landed[block].astype(jnp.float32).reshape(block_rows, LANES)
+        wide[block * block_rows : (block + 1) * block_rows, :] = these
+        flat[block * block_rows : (block + 1) * block_rows, :] = these.astype(jnp.bfloat16)
 
     far_rows = far_all.reshape(offsets, rows * SUBLANES, LANES)
     for ray in range(SUBLANES):
@@ -202,20 +207,19 @@
                 :, offset * LANES : (offset + 1) * LANES
             ]
 
-    for block in range(n_tm):
-        low = block * block_rows
-        pair = jnp.concatenate(
-            [
-                wide[low : low + block_rows, :].astype(jnp.bfloat16),
-                wide[low + block_rows : low + 2 * block_rows, :].astype(jnp.bfloat16),
-            ],
-            axis=1,
+    for tile in range(0, slots, 2):
+        taken = min(2, slots - tile)
+        products = jnp.dot(
+            jnp.concatenate(
+                [flat[0 : n_tm * block_rows, :], flat[block_rows:, :]], axis=1
+            ),
+            near_mats[:, tile * LANES : (tile + taken) * LANES],
+            preferred_element_type=jnp.float32,
         )
-        products = jnp.dot(pair, near_mats[...], preferred_element_type=jnp.float32)
-        for slot in range(slots):
-            near_all[slot, block * boxes : (block + 1) * boxes] = products[
-                :, slot * LANES : (slot + 1) * LANES
-            ].reshape(boxes, SUBLANES, LANES)
+        for nth in range(taken):
+            near_all[tile + nth] = products[:, nth * LANES : (nth + 1) * LANES].reshape(
+                rows, SUBLANES, LANES
+            )
 
     def selected(all_ref, table, count, box, block, by_slot):
         total = None
@@ -241,7 +245,7 @@
             if dt or ds:
                 pltpu.make_async_remote_copy(
                     src_ref=leaving.at[to_tm, to_boxes],
-                    dst_ref=out_ref.at[mine],
+                    dst_ref=out_ref.at[:, mine],
                     send_sem=out_send,
                     recv_sem=out_recv,
                     device_id=(to_tm, to_space),
@@ -249,10 +253,9 @@
                 ).start()
             else:
                 pltpu.make_async_copy(
-                    leaving.at[tm, to_boxes], out_ref.at[mine], out_recv
+                    leaving.at[tm, to_boxes], out_ref.at[:, mine], out_recv
                 ).start()
 
-    order = sorted(range(n_space), key=lambda ds: -min(ds, n_space - ds))
     for nth, ds in enumerate(order):
         finish(wrapped(space + ds, n_space))
         if nth:
@@ -276,13 +279,14 @@
     hbm = pl.BlockSpec(memory_space=pltpu.HBM)
     field = pl.pallas_call(
         functools.partial(fused_kernel, n_tm, n_space),
-        out_shape=jax.ShapeDtypeStruct((peers, box_dev, SUBLANES, samples), jnp.bfloat16),
+        out_shape=pltpu.VMEM(grouped.shape, jnp.bfloat16),
         in_specs=[hbm] * 5,
         out_specs=pl.BlockSpec(memory_space=pl.ANY),
         scratch_shapes=[
             pltpu.VMEM((peers, box_dev, SUBLANES, LANES), jnp.bfloat16),
             pltpu.VMEM((n_tm + 1, boxes, SUBLANES, LANES), jnp.bfloat16),
             pltpu.VMEM(((rows + boxes) * SUBLANES, LANES), jnp.float32),
+            pltpu.VMEM(((rows + boxes) * SUBLANES, LANES), jnp.bfloat16),
             pltpu.VMEM((offsets, SUBLANES, LANES), jnp.float32),
             pltpu.VMEM((slots, LANES), jnp.float32),
             pltpu.VMEM((SUBLANES, 2 * LANES, offsets * LANES), jnp.bfloat16),
@@ -300,10 +304,10 @@
             pltpu.SemaphoreType.DMA((box_dev,)),
         ],
         compiler_params=pltpu.CompilerParams(
-            collective_id=0, has_side_effects=True, vmem_limit_bytes=67043328
+            collective_id=0, has_side_effects=True, vmem_limit_bytes=60*1024*1024
         ),
-    )(grouped, source_boxes, near_boxes.T, trans_kernel, near_kernel)
-    return field.transpose(1, 0, 2, 3).reshape(signal.shape)
+    )(*[pltpu.with_memory_space_constraint(x, pltpu.HBM) for x in (grouped, source_boxes, near_boxes.T, trans_kernel, near_kernel)])
+    return field.reshape(signal.shape)
 
 
 def routed(signal, source_boxes, near_boxes, trans_kernel, near_kernel):

time: 22.2 us -> 21 us (0.946)
  local copies, waits for them, and re-layouts: 1.58 us -> 0.66 us
  Pallas kernels: 20.4 us -> 20.1 us
    reshape x1 -> x0, local copies, waits for them, and re-layouts: 1.58 us -> none  [fused_body(): return field.transpose(1, 0, 2, 3).reshape(signal.shape)]
    unnamed x0 -> x1, local copies, waits for them, and re-layouts: none -> 0.66 us
    pallas_call x1, Pallas kernels: 20.4 us -> 20.1 us  [fused_body(): pl.pallas_call(functools.partial(fused_kernel, n_tm, n_space), out_shape=...]
where the time goes in v1:
time: 21 us; the launch traced here: 20.8 us
  Pallas kernels  20.1 us (96%)
  local copies, waits for them, and re-layouts  0.66 us (3%)
    pallas_call x1, Pallas kernels, fused_body(): pl.pallas_call(functools.partial(fused_kernel, n_tm, n_space), out_shape=...  20.1 us
    unnamed x1, local copies, waits for them, and re-layouts  0.66 us

profile of v1, /device:TPU:0, one launch (start us, length us, event | category | flops | bytes accessed | tf_op | source)
XLA Modules:
  0.0 20.8 jit_solution(18404476479243632474)
XLA Ops:
  0.0 20.1 %shard_map.55 = bf16[2,32,8,128]{3,2,1,0:T(8,128)(2,1)S(1)} custom-call(bf16[2,32,8,128]{3,2,1,0:T(8,128)(2,1)} %bitcast.4, s32[16,12]{1,0:T(8,128)} %source_ref.1, s32[8,16]{1,0:T(8,128)} %bitcast.5, f32[12,32,128]{2,1,0:T(8,128)} %trans_ref.1, f32[8,128]{1,0:T(8,128)} %kernel_ref.1), custom_call_target="tpu_custom_call" | custom-call | tf_op jit(solution)/shard_map/pallas_call | solution.py:280
  20.1 0.7 %copy.7 = bf16[2,256,128]{2,1,0:T(8,128)(2,1)} copy(bf16[2,256,128]{2,1,0:T(8,128)(2,1)S(1)} %bitcast.3) | data formatting | bytes 262144
